TPU v7x, 128 devices: a whole 4x4x4 slice. The times are simulated.
128 devices in a mesh: row: 4 (over y), col: 32 (over z, x, core).
Axes of the slice: x: 4, y: 4, z: 4, core: 2. Of those that a mesh axis runs over, the one named last changes fastest.
Arguments:
- tokens: bfloat16 [768, 8192], P('col', 'row'), may hold values from -6 to 6
- gate_weight: bfloat16 [8192, 28672], P('row', 'col'), may hold values from -0.0625 to 0.0625
- up_weight: bfloat16 [8192, 28672], P('row', 'col'), may hold values from -0.0625 to 0.0625
- down_weight: bfloat16 [28672, 8192], P('col', 'row'), may hold values from -0.03125 to 0.03125
- mask_gate: int32 [128, 448], P('row', 'col'), may hold values from 0 to 1, as said below
- mask_up: int32 [128, 448], P('row', 'col'), may hold values from 0 to 1, as said below
- mask_down: int32 [448, 128], P('col', 'row'), may hold values from 0 to 1, as said below
- cotangent: bfloat16 [768, 8192], P('col', 'row'), may hold values from -1.5 to 1.5
Outputs:
- output: bfloat16 [768, 8192], P('col', 'row')
- grad_input: bfloat16 [768, 8192], P('col', 'row')
- grad_gate: bfloat16 [8192, 28672], P('row', 'col')
- grad_up: bfloat16 [8192, 28672], P('row', 'col')
- grad_down: bfloat16 [28672, 8192], P('col', 'row')
Inputs may be any that keep to these rules, and one draw needn't show every extreme that they name: `mask_gate`: 1 where a 64 x 64 block of the weight is kept, 0 where it is pruned. `mask_up`: 1 where a 64 x 64 block of the weight is kept, 0 where it is pruned. `mask_down`: 1 where a 64 x 64 block of the weight is kept, 0 where it is pruned.
All inputs are finite; a program needn't handle non-finite values.
Results may differ from a plain program's by a relative error of at most 0.006.
Values may be sent and summed in bfloat16 or wider, within the bound.
No kernel may reach another device: no remote copies, remote signals or barrier semaphores. Data moves between devices by JAX's collectives and lax.ppermute only.
A program may use at most 128 MiB of HBM per device.

v0:
```python
import jax
import jax.numpy as jnp
from jax import lax
from jax.sharding import PartitionSpec as P

BLOCK = 64


def expand(mask):
    return jnp.repeat(jnp.repeat(mask, BLOCK, 0), BLOCK, 1).astype(jnp.bfloat16)


def contract_last(left, right):
    return lax.dot_general(
        left, right, (((1,), (1,)), ((), ())), preferred_element_type=jnp.float32
    )


def contract_first(left, right):
    return lax.dot_general(
        left, right, (((0,), (0,)), ((), ())), preferred_element_type=jnp.float32
    )


def backward_gates(dhid, gate, up):
    sigma = jax.nn.sigmoid(gate)
    dgate = (dhid * up * sigma * (1.0 + gate * (1.0 - sigma))).astype(jnp.bfloat16)
    dup = (dhid * gate * sigma).astype(jnp.bfloat16)
    return (dgate, dup)


def body(tokens, gate_weight, up_weight, down_weight, mask_gate, mask_up, mask_down, cotangent):
    keep_gate = expand(mask_gate)
    keep_up = expand(mask_up)
    keep_down = expand(mask_down)
    w_gate = gate_weight * keep_gate
    w_up = up_weight * keep_up
    w_down = down_weight * keep_down
    width = w_gate.shape[1]
    panel = lax.all_gather(tokens, "col", axis=0, tiled=True)
    stacked = jnp.concatenate([w_gate, w_up], axis=1)
    partial_both = jnp.dot(panel, stacked, preferred_element_type=jnp.float32)
    summed = lax.psum(partial_both, "row")
    gate = summed[:, :width]
    up = summed[:, width:]
    hidden = (jax.nn.silu(gate) * up).astype(jnp.bfloat16)
    output = lax.psum_scatter(
        jnp.dot(hidden, w_down, preferred_element_type=jnp.float32),
        "col",
        scatter_dimension=0,
        tiled=True,
    ).astype(jnp.bfloat16)
    cot_panel = lax.all_gather(cotangent, "col", axis=0, tiled=True)
    partial_dhid = contract_last(cot_panel, w_down)
    dhid = lax.psum(partial_dhid, "row")
    dgate, dup = backward_gates(dhid, gate, up)
    grad_down = (contract_first(hidden, cot_panel) * keep_down).astype(jnp.bfloat16)
    grad_gate = (contract_first(panel, dgate) * keep_gate).astype(jnp.bfloat16)
    grad_up = (contract_first(panel, dup) * keep_up).astype(jnp.bfloat16)
    grad_input = lax.psum_scatter(
        contract_last(dgate, w_gate) + contract_last(dup, w_up),
        "col",
        scatter_dimension=0,
        tiled=True,
    ).astype(jnp.bfloat16)
    return (output, grad_input, grad_gate, grad_up, grad_down)


def solution(mesh):
    return jax.shard_map(
        body,
        mesh=mesh,
        in_specs=(
            P("col", "row"),
            P("row", "col"),
            P("row", "col"),
            P("col", "row"),
            P("row", "col"),
            P("row", "col"),
            P("col", "row"),
            P("col", "row"),
        ),
        out_specs=(
            P("col", "row"),
            P("col", "row"),
            P("row", "col"),
            P("row", "col"),
            P("col", "row"),
        ),
        check_vma=False,
    )
```

profile of v0, /device:TPU:0, one launch (start us, length us, event | category | flops | bytes accessed | tf_op | source)
XLA Modules:
  0.0 472.1 jit_solution(7040883705480512886)
XLA Ops:
  10.7 6.1 %copy.24 = bf16[2048,896]{0,1:T(8,128)(2,1)} copy(bf16[2048,896]{1,0:T(8,128)(2,1)} %param.9) | data formatting | bytes 7340032 | tf_op args[1]
  16.7 6.1 %copy.25 = bf16[2048,896]{0,1:T(8,128)(2,1)} copy(bf16[2048,896]{1,0:T(8,128)(2,1)} %param.10) | data formatting | bytes 7340032 | tf_op args[2]
  23.2 6.1 %copy.27 = bf16[896,2048]{0,1:T(8,128)(2,1)} copy(bf16[896,2048]{1,0:T(8,128)(2,1)} %param.11) | data formatting | bytes 7340032 | tf_op args[3]
  29.2 4.4 bitcast_multiply_fusion.4
  34.8 3.6 bitcast_multiply_fusion.2
  38.4 19.5 %all-gather.5.cloned.1.call-done = bf16[768,2048]{1,0:T(8,128)(2,1)} async-done(((bf16[24,2048]{1,0:T(8,128)(2,1)}), bf16[768,2048]{1,0:T(8,128)(2,1)}) %all-gather.5.cloned.1.call-update) | async-done | bytes 3145744 | tf_op jit(solution)/shard_map/all_gather | solution.py:53
  57.9 7.6 %convolution_bitcast_fusion = f32[768,896]{0,1:T(8,128)} fusion(bf16[896,2048]{0,1:T(8,128)(2,1)} %bitcast_multiply_fusion.4, bf16[768,2048]{1,0:T(8,128)(2,1)} %all-gather.5.cloned.1.call-done), kind=kOutput, calls=%fused_computation.18 | convolution fusion | flops 2818572288 | bytes 9568256 | tf_op jit(solution)/shard_map/dot_general | solution.py:14
  65.5 39.1 %all-gather.3.cloned.1.call-done = bf16[768,2048]{1,0:T(8,128)(2,1)} async-done(((bf16[24,2048]{1,0:T(8,128)(2,1)}), bf16[768,2048]{1,0:T(8,128)(2,1)}) %all-gather.3.cloned.1.call-update) | async-done | bytes 3145744 | tf_op jit(solution)/shard_map/all_gather | solution.py:40
  104.7 12.3 %fusion.6 = f32[768,1792]{0,1:T(8,128)} fusion(bf16[768,2048]{1,0:T(8,128)(2,1)} %all-gather.3.cloned.1.call-done, bf16[2048,896]{0,1:T(8,128)(2,1)} %get-tuple-element.25, bf16[2048,896]{0,1:T(8,128)(2,1)} %get-tuple-element.26), kind=kOutput, calls=%fused_computation.11 | convolution fusion | flops 5651824640 | bytes 15990784 | tf_op jit(solution)/shard_map/dot_general | solution.py:42
  117.3 157.7 %all-reduce.3.cloned.1.call-done = (f32[768,1792]{0,1:T(8,128)}, f32[768,896]{0,1:T(8,128)}) async-done(((f32[768,1792]{0,1:T(8,128)}, f32[768,896]{0,1:T(8,128)}), (f32[768,1792]{0,1:T(8,128)}, f32[768,896]{0,1:T(8,128)})) %all-reduce.3.cloned.1.call-update) | async-done | bytes 8257552 | tf_op jit(solution)/shard_map/psum | solution.py:43
  274.9 4.3 multiply_convert_fusion.1
  279.4 3.5 fusion.11
  283.0 5.4 %convolution_add_fusion = f32[768,2048]{1,0:T(8,128)} fusion(f32[768,2048]{1,0:T(8,128)S(1)} %fusion.11, bf16[768,896]{0,1:T(8,128)(2,1)S(1)} %get-tuple-element.22, bf16[2048,896]{0,1:T(8,128)(2,1)S(1)} %copy-done.2), kind=kOutput, calls=%fused_computation.12 | convolution fusion | flops 2820145152 | bytes 17629184 | tf_op jit(solution)/shard_map/dot_general | solution.py:14
  288.4 7.4 %fusion.10 = f32[768,2048]{1,0:T(8,128)} fusion(bf16[768,896]{0,1:T(8,128)(2,1)S(1)} %get-tuple-element.24, bf16[896,2048]{0,1:T(8,128)(2,1)} %bitcast_multiply_fusion.4), kind=kOutput, calls=%fused_computation.20 | convolution fusion | flops 2818572288 | bytes 11337728 | tf_op jit(solution)/shard_map/dot_general | solution.py:48
  295.9 2.1 broadcast_in_dim.23
  298.0 6.2 %copy.28 = bf16[896,2048]{1,0:T(8,128)(2,1)} copy(bf16[896,2048]{0,1:T(8,128)(2,1)} %bitcast.41) | data formatting | bytes 7340032 | tf_op jit(solution)/shard_map/convert_element_type | solution.py:10
  304.2 7.3 %fusion.5 = bf16[2048,896]{0,1:T(8,128)(2,1)} fusion(bf16[768,896]{0,1:T(8,128)(2,1)} %copy-done.4, bf16[768,2048]{1,0:T(8,128)(2,1)} %all-gather.3.cloned.1.call-done, bf16[2048,14]{0,1:T(8,128)(2,1)S(1)} %convert_element_type.67), kind=kOutput, calls=%fused_computation.7 | convolution fusion | flops 2824077312 | bytes 8249344 | tf_op jit(solution)/shard_map/dot_general | solution.py:20
  311.5 6.2 %copy.29 = bf16[2048,896]{1,0:T(8,128)(2,1)} copy(bf16[2048,896]{0,1:T(8,128)(2,1)} %fusion.5) | data formatting | bytes 7340032
  317.7 6.9 %fusion.4 = bf16[2048,896]{0,1:T(8,128)(2,1)} fusion(bf16[768,896]{0,1:T(8,128)(2,1)S(1)} %get-tuple-element.22, bf16[768,2048]{1,0:T(8,128)(2,1)} %all-gather.3.cloned.1.call-done, bf16[2048,14]{0,1:T(8,128)(2,1)S(1)} %convert_element_type.70), kind=kOutput, calls=%fused_computation.5 | convolution fusion | flops 2824077312 | bytes 8249344 | tf_op jit(solution)/shard_map/dot_general | solution.py:20
  324.6 6.1 %copy.30 = bf16[2048,896]{1,0:T(8,128)(2,1)} copy(bf16[2048,896]{0,1:T(8,128)(2,1)} %fusion.4) | data formatting | bytes 7340032
  330.6 6.9 %multiply_convert_fusion = bf16[896,2048]{1,0:T(8,128)(2,1)} fusion(bf16[896,2048]{1,0:T(8,128)(2,1)} %copy.28, bf16[768,896]{0,1:T(8,128)(2,1)S(1)} %get-tuple-element.24, bf16[768,2048]{1,0:T(8,128)(2,1)} %all-gather.5.cloned.1.call-done), kind=kOutput, calls=%fused_computation.8 | convolution fusion | flops 2824077312 | bytes 11862016 | tf_op jit(solution)/shard_map/dot_general | solution.py:20
  337.5 37.2 %reduce-scatter.5.cloned.1.call-done = f32[24,2048]{1,0:T(8,128)} async-done(((f32[768,2048]{1,0:T(8,128)}), f32[24,2048]{1,0:T(8,128)}) %reduce-scatter.5.cloned.1.call-update) | async-done | bytes 196624 | tf_op jit(solution)/shard_map/reduce_scatter | solution.py:60
  374.8 1.6 convert_element_type.79
  376.3 87.7 %reduce-scatter.3.cloned.1.call-done = f32[24,2048]{1,0:T(8,128)} async-done(((f32[768,2048]{1,0:T(8,128)}), f32[24,2048]{1,0:T(8,128)}) %reduce-scatter.3.cloned.1.call-update) | async-done | bytes 196624 | tf_op jit(solution)/shard_map/reduce_scatter | solution.py:47
  (33 shorter events, 7.0 us)
Async XLA Ops:
  7.2 50.8 %all-gather.5.cloned.1.call-start = ((), (), s32[]{:S(2)}) async-start(), calls=%async_computation.4 | async-start | bytes 3244032 | tf_op jit(solution)/shard_map/all_gather | solution.py:53
  7.9 96.8 %all-gather.3.cloned.1.call-start = ((), (), s32[]{:S(2)}) async-start(), calls=%async_computation.2 | async-start | bytes 3244032 | tf_op jit(solution)/shard_map/all_gather | solution.py:40
  8.6 266.3 %all-reduce.3.cloned.1.call-start = ((), (), s32[]{:S(2)}) async-start(), calls=%async_computation.6 | async-start | bytes 16515072 | tf_op jit(solution)/shard_map/psum | solution.py:43
  16.7 6.1 %copy-start.5 = (s32[14,32]{1,0:T(8,128)S(1)}, s32[14,32]{1,0:T(8,128)}, u32[]{:S(2)}) copy-start(s32[14,32]{1,0:T(8,128)} %param.14) | copy-start | bytes 5380
  29.2 4.4 copy-start
  29.2 5.6 %copy-start.1 = (bf16[2048,896]{0,1:T(8,128)(2,1)S(1)}, bf16[2048,896]{0,1:T(8,128)(2,1)}, u32[]{:S(2)}) copy-start(bf16[2048,896]{0,1:T(8,128)(2,1)} %copy.25) | copy-start | bytes 11010052
  117.0 257.7 %reduce-scatter.5.cloned.1.call-start = ((), (), s32[]{:S(2)}) async-start(), calls=%async_computation.5 | async-start | bytes 6488064 | tf_op jit(solution)/shard_map/reduce_scatter | solution.py:60
  274.9 4.5 copy-start.3
  279.2 3.7 copy-start.4
  279.4 3.5 copy-start.2
  288.4 175.6 %reduce-scatter.3.cloned.1.call-start = ((), (), s32[]{:S(2)}) async-start(), calls=%async_computation.3 | async-start | bytes 6488064 | tf_op jit(solution)/shard_map/reduce_scatter | solution.py:47
Sparse Core Ops, SparseCore 0:
  10.3 47.6 all-gather.4
  60.2 44.4 all-gather.2
  117.2 157.7 all-reduce.2
  288.5 86.2 reduce-scatter.4
  378.3 85.6 reduce-scatter.2
where the time goes:
time: 473 us; the launch traced here: 472 us
  waiting for transfers between devices  343 us (73%)
  matrix products  57.4 us (12%)
  local copies, waits for them, and re-layouts  40.9 us (9%)
  other arithmetic  16.9 us (4%)
  between operations  13.9 us (3%)
    psum x1, waiting for transfers between devices, body(): summed = lax.psum(partial_both, 'row')  158 us
    reduce_scatter x1, waiting for transfers between devices, body(): lax.psum_scatter(jnp.dot(hidden, w_down, preferred_element_type=jnp.float...  87.7 us
    all_gather x1, waiting for transfers between devices, body(): panel = lax.all_gather(tokens, 'col', axis=0, tiled=True)  39.1 us
    reduce_scatter x1, waiting for transfers between devices, body(): lax.psum_scatter(contract_last(dgate, w_gate) + contract_last(dup, w_up),...  37.2 us
    unnamed x17, local copies, waits for them, and re-layouts  31.7 us
    dot_general x3, matrix products, contract_first(): lax.dot_general(left, right, (((0,), (0,)), ((), ())), preferred_element_...  21.1 us
    all_gather x1, waiting for transfers between devices, body(): cot_panel = lax.all_gather(cotangent, 'col', axis=0, tiled=True)  19.5 us
    dot_general x3, matrix products, contract_last(): lax.dot_general(left, right, (((1,), (1,)), ((), ())), preferred_element_...  16.5 us
  transfers between devices with their start and end apart: 5, of which 5 were waited for; matrix products, arithmetic and copies ran while one was open for 18% of the time, Pallas kernels for 0%

commit v1 on v0

--- a/solution.py
+++ b/solution.py
@@ -4,6 +4,13 @@
 from jax.sharding import PartitionSpec as P
 
 BLOCK = 64
+
+
+def find_flows_all(shard_in, named_axis):
+    reached = jnp.stack([shard_in for _ in range(jax.lax.axis_size(named_axis))])
+    e_next = jax.lax.all_to_all(reached, axis_name=named_axis, concat_axis=0, split_axis=0)
+    z1 = jnp.concatenate(e_next, axis=0)
+    return z1
 
 
 def expand(mask):
@@ -50,7 +57,7 @@
         scatter_dimension=0,
         tiled=True,
     ).astype(jnp.bfloat16)
-    cot_panel = lax.all_gather(cotangent, "col", axis=0, tiled=True)
+    cot_panel = find_flows_all(cotangent, "col")
     partial_dhid = contract_last(cot_panel, w_down)
     dhid = lax.psum(partial_dhid, "row")
     dgate, dup = backward_gates(dhid, gate, up)

time: 473 us -> 451 us (0.953)
  waiting for transfers between devices: 343 us -> 309 us
  starting transfers between devices: 0.38 us -> 8.72 us
    all_gather x1, waiting for transfers between devices: 39.1 us -> 12.5 us  [body(): panel = lax.all_gather(tokens, 'col', axis=0, tiled=True)]
    all_gather x1 -> x0, waiting for transfers between devices: 19.5 us -> none  [body(): cot_panel = lax.all_gather(cotangent, 'col', axis=0, tiled=True)]
    all_to_all x0 -> x1, waiting for transfers between devices: none -> 14.4 us  [find_flows_all(): jax.lax.all_to_all(reached, axis_name=named_axis, concat_axis=0, split_ax...]
    all_to_all x0 -> x1, starting transfers between devices: none -> 8.38 us  [find_flows_all(): jax.lax.all_to_all(reached, axis_name=named_axis, concat_axis=0, split_ax...]
    unnamed x17 -> x23, local copies, waits for them, and re-layouts: 31.7 us -> 31.7 us
  transfers between devices with their start and end apart: 5 -> 5, of which waited for: 5 -> 5; matrix products, arithmetic and copies ran while one was open for 18% -> 20% of each run, Pallas kernels for 0% -> 0%
where the time goes in v1:
time: 451 us; the launch traced here: 450 us
  waiting for transfers between devices  309 us (69%)
  matrix products  57.7 us (13%)
  local copies, waits for them, and re-layouts  43.9 us (10%)
  other arithmetic  16.3 us (4%)
  between operations  13.9 us (3%)
  starting transfers between devices  8.72 us (2%)
    psum x1, waiting for transfers between devices, body(): summed = lax.psum(partial_both, 'row')  158 us
    reduce_scatter x1, waiting for transfers between devices, body(): lax.psum_scatter(jnp.dot(hidden, w_down, preferred_element_type=jnp.float...  87.6 us
    reduce_scatter x1, waiting for transfers between devices, body(): lax.psum_scatter(contract_last(dgate, w_gate) + contract_last(dup, w_up),...  36.1 us
    unnamed x23, local copies, waits for them, and re-layouts  31.7 us
    dot_general x3, matrix products, contract_first(): lax.dot_general(left, right, (((0,), (0,)), ((), ())), preferred_element_...  21 us
    dot_general x3, matrix products, contract_last(): lax.dot_general(left, right, (((1,), (1,)), ((), ())), preferred_element_...  15.7 us
    all_to_all x1, waiting for transfers between devices, find_flows_all(): jax.lax.all_to_all(reached, axis_name=named_axis, concat_axis=0, split_ax...  14.4 us
    all_gather x1, waiting for transfers between devices, body(): panel = lax.all_gather(tokens, 'col', axis=0, tiled=True)  12.5 us
  transfers between devices with their start and end apart: 5, of which 5 were waited for; matrix products, arithmetic and copies ran while one was open for 20% of the time, Pallas kernels for 0%

profile of v1, /device:TPU:0, one launch (start us, length us, event | category | flops | bytes accessed | tf_op | source)
XLA Modules:
  0.0 449.6 jit_solution(3770028686427340977)
XLA Ops:
  7.9 2.9 stack.2
  10.8 8.4 %all-to-all-start = ((bf16[32,24,2048]{2,1,0:T(8,128)(2,1)}), bf16[32,24,2048]{2,1,0:T(8,128)(2,1)S(1)}, u32[]{:S(2)}, u32[]{:S(2)}) async-start(bf16[32,24,2048]{2,1,0:T(8,128)(2,1)} %stack.2), calls=%async_computation.1 | async-start | bytes 6291456 | tf_op jit(solution)/shard_map/all_to_all | solution.py:11
  19.9 6.1 %copy.24 = bf16[2048,896]{0,1:T(8,128)(2,1)} copy(bf16[2048,896]{1,0:T(8,128)(2,1)} %param.9) | data formatting | bytes 7340032 | tf_op args[1]
  25.9 6.1 %copy.25 = bf16[2048,896]{0,1:T(8,128)(2,1)} copy(bf16[2048,896]{1,0:T(8,128)(2,1)} %param.10) | data formatting | bytes 7340032 | tf_op args[2]
  32.4 6.1 %copy.27 = bf16[896,2048]{0,1:T(8,128)(2,1)} copy(bf16[896,2048]{1,0:T(8,128)(2,1)} %param.11) | data formatting | bytes 7340032 | tf_op args[3]
  38.5 4.4 bitcast_multiply_fusion.4
  44.1 3.6 bitcast_multiply_fusion.2
  47.7 14.4 %all-to-all-done = bf16[32,24,2048]{2,1,0:T(8,128)(2,1)S(1)} async-done(((bf16[32,24,2048]{2,1,0:T(8,128)(2,1)}), bf16[32,24,2048]{2,1,0:T(8,128)(2,1)S(1)}, u32[]{:S(2)}, u32[]{:S(2)}) %all-to-all-start) | async-done | bytes 3145760 | tf_op jit(solution)/shard_map/all_to_all | solution.py:11
  62.1 6.7 %convolution_bitcast_fusion = f32[768,896]{0,1:T(8,128)} fusion(bf16[896,2048]{0,1:T(8,128)(2,1)} %bitcast_multiply_fusion.4, bf16[768,2048]{1,0:T(8,128)(2,1)S(1)} %bitcast.43), kind=kOutput, calls=%fused_computation.18 | convolution fusion | flops 2818572288 | bytes 9568256 | tf_op jit(solution)/shard_map/dot_general | solution.py:21
  68.8 12.5 %all-gather.2.cloned.1.call-done = bf16[768,2048]{1,0:T(8,128)(2,1)} async-done(((bf16[24,2048]{1,0:T(8,128)(2,1)}), bf16[768,2048]{1,0:T(8,128)(2,1)}) %all-gather.2.cloned.1.call-update) | async-done | bytes 3145744 | tf_op jit(solution)/shard_map/all_gather | solution.py:47
  81.3 12.4 %fusion.6 = f32[768,1792]{0,1:T(8,128)} fusion(bf16[768,2048]{1,0:T(8,128)(2,1)} %all-gather.2.cloned.1.call-done, bf16[2048,896]{0,1:T(8,128)(2,1)} %get-tuple-element.25, bf16[2048,896]{0,1:T(8,128)(2,1)} %get-tuple-element.26), kind=kOutput, calls=%fused_computation.11 | convolution fusion | flops 5651824640 | bytes 15990784 | tf_op jit(solution)/shard_map/dot_general | solution.py:49
  94.0 157.7 %all-reduce.3.cloned.1.call-done = (f32[768,1792]{0,1:T(8,128)}, f32[768,896]{0,1:T(8,128)}) async-done(((f32[768,1792]{0,1:T(8,128)}, f32[768,896]{0,1:T(8,128)}), (f32[768,1792]{0,1:T(8,128)}, f32[768,896]{0,1:T(8,128)})) %all-reduce.3.cloned.1.call-update) | async-done | bytes 8257552 | tf_op jit(solution)/shard_map/psum | solution.py:50
  251.7 5.1 %multiply_convert_fusion.1 = (bf16[768,896]{0,1:T(8,128)(2,1)S(1)}, bf16[768,896]{0,1:T(8,128)(2,1)S(1)}, bf16[768,896]{0,1:T(8,128)(2,1)}) fusion(f32[768,896]{0,1:T(8,128)} %get-tuple-element.21, f32[768,1792]{0,1:T(8,128)} %get-tuple-element.20), kind=kLoop, calls=%fused_computation.13 | loop fusion | flops 11010048 | bytes 12386304 | tf_op jit(solution)/shard_map/convert_element_type | solution.py:35
  256.8 3.5 fusion.11
  260.4 5.4 %convolution_add_fusion = f32[768,2048]{1,0:T(8,128)} fusion(f32[768,2048]{1,0:T(8,128)S(1)} %fusion.11, bf16[768,896]{0,1:T(8,128)(2,1)S(1)} %get-tuple-element.22, bf16[2048,896]{0,1:T(8,128)(2,1)S(1)} %copy-done.2), kind=kOutput, calls=%fused_computation.12 | convolution fusion | flops 2820145152 | bytes 17629184 | tf_op jit(solution)/shard_map/dot_general | solution.py:21
  265.9 8.6 %fusion.10 = f32[768,2048]{1,0:T(8,128)} fusion(bf16[768,896]{0,1:T(8,128)(2,1)} %get-tuple-element.24, bf16[896,2048]{0,1:T(8,128)(2,1)} %bitcast_multiply_fusion.4), kind=kOutput, calls=%fused_computation.20 | convolution fusion | flops 2818572288 | bytes 11337728 | tf_op jit(solution)/shard_map/dot_general | solution.py:55
  276.6 6.3 %copy.28 = bf16[896,2048]{1,0:T(8,128)(2,1)} copy(bf16[896,2048]{0,1:T(8,128)(2,1)} %bitcast.42) | data formatting | bytes 7340032 | tf_op jit(solution)/shard_map/convert_element_type | solution.py:17
  282.9 7.3 %fusion.5 = bf16[2048,896]{0,1:T(8,128)(2,1)} fusion(bf16[768,896]{0,1:T(8,128)(2,1)} %copy-done.5, bf16[768,2048]{1,0:T(8,128)(2,1)} %all-gather.2.cloned.1.call-done, bf16[2048,14]{0,1:T(8,128)(2,1)S(1)} %convert_element_type.67), kind=kOutput, calls=%fused_computation.7 | convolution fusion | flops 2824077312 | bytes 8249344 | tf_op jit(solution)/shard_map/dot_general | solution.py:27
  290.2 6.2 %copy.29 = bf16[2048,896]{1,0:T(8,128)(2,1)} copy(bf16[2048,896]{0,1:T(8,128)(2,1)} %fusion.5) | data formatting | bytes 7340032
  296.5 7.3 %fusion.4 = bf16[2048,896]{0,1:T(8,128)(2,1)} fusion(bf16[768,896]{0,1:T(8,128)(2,1)} %copy-done.4, bf16[768,2048]{1,0:T(8,128)(2,1)} %all-gather.2.cloned.1.call-done, bf16[2048,14]{0,1:T(8,128)(2,1)S(1)} %convert_element_type.70), kind=kOutput, calls=%fused_computation.5 | convolution fusion | flops 2824077312 | bytes 8249344 | tf_op jit(solution)/shard_map/dot_general | solution.py:27
  303.8 6.0 %copy.30 = bf16[2048,896]{1,0:T(8,128)(2,1)} copy(bf16[2048,896]{0,1:T(8,128)(2,1)} %fusion.4) | data formatting | bytes 7340032
  309.9 6.3 %multiply_convert_fusion = bf16[896,2048]{1,0:T(8,128)(2,1)} fusion(bf16[896,2048]{1,0:T(8,128)(2,1)} %copy.28, bf16[768,896]{0,1:T(8,128)(2,1)} %get-tuple-element.24, bf16[768,2048]{1,0:T(8,128)(2,1)S(1)} %bitcast.44), kind=kOutput, calls=%fused_computation.8 | convolution fusion | flops 2824077312 | bytes 11862016 | tf_op jit(solution)/shard_map/dot_general | solution.py:27
  316.2 36.1 %reduce-scatter.5.cloned.1.call-done = f32[24,2048]{1,0:T(8,128)} async-done(((f32[768,2048]{1,0:T(8,128)}), f32[24,2048]{1,0:T(8,128)}) %reduce-scatter.5.cloned.1.call-update) | async-done | bytes 196624 | tf_op jit(solution)/shard_map/reduce_scatter | solution.py:67
  353.8 87.6 %reduce-scatter.3.cloned.1.call-done = f32[24,2048]{1,0:T(8,128)} async-done(((f32[768,2048]{1,0:T(8,128)}), f32[24,2048]{1,0:T(8,128)}) %reduce-scatter.3.cloned.1.call-update) | async-done | bytes 196624 | tf_op jit(solution)/shard_map/reduce_scatter | solution.py:54
  (39 shorter events, 8.5 us)
Async XLA Ops:
  7.2 74.1 %all-gather.2.cloned.1.call-start = ((), (), s32[]{:S(2)}) async-start(), calls=%async_computation.3 | async-start | bytes 3244032 | tf_op jit(solution)/shard_map/all_gather | solution.py:47
  10.8 8.4 %copy-start.6 = (s32[32,14]{0,1:T(8,128)S(1)}, s32[32,14]{0,1:T(8,128)}, u32[]{:S(2)}) copy-start(s32[32,14]{0,1:T(8,128)} %param.12) | copy-start | bytes 5380
  10.8 8.7 %copy-start.7 = (s32[32,14]{0,1:T(8,128)S(1)}, s32[32,14]{0,1:T(8,128)}, u32[]{:S(2)}) copy-start(s32[32,14]{0,1:T(8,128)} %param.13) | copy-start | bytes 5380
  10.8 51.2 %all-to-all-start = ((bf16[32,24,2048]{2,1,0:T(8,128)(2,1)}), bf16[32,24,2048]{2,1,0:T(8,128)(2,1)S(1)}, u32[]{:S(2)}, u32[]{:S(2)}) async-start(bf16[32,24,2048]{2,1,0:T(8,128)(2,1)} %stack.2), calls=%async_computation.1 | async-start | bytes 6291456 | tf_op jit(solution)/shard_map/all_to_all | solution.py:11
  19.2 232.4 %all-reduce.3.cloned.1.call-start = ((), (), s32[]{:S(2)}) async-start(), calls=%async_computation.6 | async-start | bytes 16515072 | tf_op jit(solution)/shard_map/psum | solution.py:50
  25.9 6.1 %copy-start.8 = (s32[14,32]{1,0:T(8,128)S(1)}, s32[14,32]{1,0:T(8,128)}, u32[]{:S(2)}) copy-start(s32[14,32]{1,0:T(8,128)} %param.14) | copy-start | bytes 5380
  38.5 4.4 copy-start
  38.5 5.6 %copy-start.1 = (bf16[2048,896]{0,1:T(8,128)(2,1)S(1)}, bf16[2048,896]{0,1:T(8,128)(2,1)}, u32[]{:S(2)}) copy-start(bf16[2048,896]{0,1:T(8,128)(2,1)} %copy.25) | copy-start | bytes 11010052
  93.7 258.5 %reduce-scatter.5.cloned.1.call-start = ((), (), s32[]{:S(2)}) async-start(), calls=%async_computation.5 | async-start | bytes 6488064 | tf_op jit(solution)/shard_map/reduce_scatter | solution.py:67
  251.6 5.2 %copy-start.3 = (bf16[2048,896]{0,1:T(8,128)(2,1)S(1)}, bf16[2048,896]{0,1:T(8,128)(2,1)}, u32[]{:S(2)}) copy-start(bf16[2048,896]{0,1:T(8,128)(2,1)} %get-tuple-element.26) | copy-start | bytes 11010052
  256.8 3.6 copy-start.5
  256.8 3.6 copy-start.4
  256.8 3.6 copy-start.2
  265.8 175.6 %reduce-scatter.3.cloned.1.call-start = ((), (), s32[]{:S(2)}) async-start(), calls=%async_computation.4 | async-start | bytes 6488064 | tf_op jit(solution)/shard_map/reduce_scatter | solution.py:54
Sparse Core Ops, SparseCore 0:
  10.3 70.9 all-gather.1
  93.9 157.7 all-reduce.2
  266.0 86.2 reduce-scatter.4
  355.8 85.5 reduce-scatter.2
